TPU v7x, 32 devices: a whole 2x2x4 slice. The times are simulated.
32 devices in a mesh: wide: 8 (over z, x), bulk: 4 (over y, core).
Axes of the slice: x: 2, y: 2, z: 4, core: 2. Of those that a mesh axis runs over, the one named last changes fastest.
Arguments:
- fields: float32 [1024, 6, 512], P(('wide', 'bulk')), may hold values from -6 to 6
- scales: float32 [1024, 3], P(('wide', 'bulk')), may hold values from 1 to 3
- class_table: float32 [8, 2], replicated, may hold values from 1 to 4
- material: int32 [1024], P(('wide', 'bulk')), may hold values from 0 to 7, as said below
- neighbour_class: int32 [1024, 6], P(('wide', 'bulk')), may hold values from 0 to 7, as said below
- orientation: int32 [1024, 6], P(('wide', 'bulk')), may hold values from 0 to 7
- face_source: int32 [1024, 6], P(('wide', 'bulk')), may hold values from -1 to 287, as said below
- wide_send: int32 [8, 4, 4, 16], P('wide', 'bulk'), may hold values from -1 to 191, as said below
- bulk_send: int32 [8, 4, 2, 16], P('wide', 'bulk'), may hold values from -1 to 191, as said below
Outputs:
- new_fields: float32 [1024, 6, 512], P(('wide', 'bulk'))
Inputs may be any that keep to these rules, and one draw needn't show every extreme that they name: `material`: classes of elements; class 0 and class 7 occur in every draw. `neighbour_class`: for a face whose source is an own face or a received trace row, the material class of the element that trace belongs to; for a boundary face, the element's own class. `face_source`: rows 0 .. 191 are the device's own faces, the next 64 rows what arrived over wide (16 for each offset -2, -1, +1, +2 in order), then 16 rows from the previous and 16 from the next index of bulk. Every received row that carries a trace is named by exactly one face of the receiving device, rows from -1 entries by none; no face names itself; some faces are boundary faces. `wide_send`: Element-face numbers of the sending device; a device shares faces over wide only with the indices at offsets -2, -1, +1 and +2 (cyclic); in each block of 16 entries the used entries come first and -1 fills the rest; every block holds at least one entry, and every device fills all 16 entries for offset +1. `bulk_send`: Element-face numbers of the sending device; used entries first, then -1; every row holds at least one entry and some rows of every draw are full.
All inputs are finite; a program needn't handle non-finite values.
Results may differ from a plain program's by a relative error of at most 0.00005.
Values sent between devices are 32-bit elements; how exact they have to be, the bound alone decides.
A program may use at most 64 MiB of HBM per device.

v0:
```python
import jax
import jax.numpy as jnp
import numpy as np
from jax import lax
from jax.sharding import PartitionSpec as P

TIME_STEP = 0.005
LIFT_WEIGHT = 28.0


def from_behind(value, axis, steps):
    count = lax.axis_size(axis)
    pairs = [(source, (source + steps) % count) for source in range(count)]
    return lax.ppermute(value, axis, pairs)


def legendre_value(degree, point):
    previous = 1.0
    current = point
    for order in range(1, degree):
        following = ((2 * order + 1) * point * current - order * previous) / (order + 1)
        previous = current
        current = following
    return current


def gll_numpy():
    degree = 7
    points = [
        -1.0,
        -0.8717401485096066,
        -0.5917001814331423,
        -0.2092992179024789,
        0.2092992179024789,
        0.5917001814331423,
        0.8717401485096066,
        1.0,
    ]
    values = [legendre_value(degree, point) for point in points]
    matrix = np.zeros((degree + 1, degree + 1))
    for row_index in range(degree + 1):
        for col_index in range(degree + 1):
            if row_index != col_index:
                matrix[row_index, col_index] = values[row_index] / (
                    values[col_index] * (points[row_index] - points[col_index])
                )
    matrix[0, 0] = -degree * (degree + 1) / 4.0
    matrix[degree, degree] = degree * (degree + 1) / 4.0
    return matrix


def derive_table():
    matrix = gll_numpy().T
    identity = np.eye(8)
    first = np.kron(np.kron(matrix, identity), identity)
    second = np.kron(np.kron(identity, matrix), identity)
    third = np.kron(np.kron(identity, identity), matrix)
    return jnp.asarray(np.concatenate([first, second, third], axis=1), dtype=jnp.float32)


def face_nodes():
    nodes = np.zeros((6, 64), dtype=np.int64)
    for face in range(6):
        axis_id = face // 2
        level = 7 * (face % 2)
        for place in range(64):
            outer = place // 8
            inner = place % 8
            if axis_id == 0:
                coords = (level, outer, inner)
            elif axis_id == 1:
                coords = (outer, level, inner)
            else:
                coords = (outer, inner, level)
            nodes[face, place] = 64 * coords[0] + 8 * coords[1] + coords[2]
    return nodes


def lookup(indices, values):
    onehot = indices[..., None] == jnp.arange(values.shape[0], dtype=jnp.int32)
    return jnp.sum(jnp.where(onehot, values, 0.0), axis=-1)


def cross_with(normal, first, second, third):
    return (
        normal[1] * third - normal[2] * second,
        normal[2] * first - normal[0] * third,
        normal[0] * second - normal[1] * first,
    )


def pick_rows(traces, index):
    got = jnp.take(traces, jnp.maximum(index, 0), axis=0)
    return jnp.where((index >= 0)[:, None], got, 0.0)


def near_shift(payload, offset):
    return from_behind(payload, "wide", offset)


def bulk_shift(payload, offset):
    return from_behind(payload, "bulk", offset)


def local(
    fields,
    scales,
    class_table,
    material,
    neighbour_class,
    orientation,
    face_source,
    wide_send,
    bulk_send,
):
    elems = fields.shape[0]
    faces = 6 * elems
    nodes = face_nodes()
    trace_index = jnp.asarray(
        (np.arange(6)[None, :, None] * 512 + nodes[:, None, :]).reshape(-1), dtype=jnp.int32
    )
    lift_table = np.zeros((384, 512))
    lift_table[np.arange(384), nodes.reshape(-1)] = 1.0
    lift_table = jnp.asarray(lift_table, dtype=jnp.float32)
    slopes_table = derive_table()
    col_face = np.arange(384) // 64
    col_axis = col_face // 2
    col_sign = 2.0 * (col_face % 2) - 1.0
    normal = [
        jnp.asarray(np.where(col_axis == dim, col_sign, 0.0), dtype=jnp.float32) for dim in range(3)
    ]
    col_axis_j = jnp.asarray(col_axis, dtype=jnp.int32)
    col_face_j = jnp.asarray(col_face, dtype=jnp.int32)
    sign_cols = jnp.asarray(
        np.repeat(np.array([-1.0, -1.0, -1.0, 1.0, 1.0, 1.0]), 64), dtype=jnp.float32
    )
    wide_list = wide_send.reshape(-1)
    bulk_list = bulk_send.reshape(-1)
    imped_table = jnp.sqrt(class_table[:, 1] / class_table[:, 0])
    permit = lookup(material, class_table[:, 0])[:, None]
    permea = lookup(material, class_table[:, 1])[:, None]
    own_imp = lookup(material, imped_table)[:, None]
    outside_imp = lookup(neighbour_class, imped_table)
    z_out = jnp.take(outside_imp, col_face_j, axis=1)
    lift = LIFT_WEIGHT * jnp.take(scales, col_axis_j, axis=1)
    e_factor = -lift / (permit * (own_imp + z_out))
    h_factor = lift / (permea * (1.0 / own_imp + 1.0 / z_out))
    source_rows = jnp.maximum(face_source, 0).reshape(-1)
    flags = orientation.reshape(-1, 1)
    place = jnp.arange(64, dtype=jnp.int32)[None, :]
    outer = place // 8
    inner = place % 8
    outer_new = jnp.where(flags & 1 > 0, 7 - outer, outer)
    inner_new = jnp.where(flags & 2 > 0, 7 - inner, inner)
    within = jnp.where(flags & 4 > 0, inner_new * 8 + outer_new, outer_new * 8 + inner_new)
    turn_index = (jnp.arange(6, dtype=jnp.int32)[None, :, None] * 64 + within[:, None, :]).reshape(
        faces, 384
    )
    boundary = (face_source.reshape(-1) < 0)[:, None]

    def rate_of(state):
        traces = jnp.take(state.reshape(elems, 3072), trace_index, axis=1).reshape(faces, 384)
        sent = pick_rows(traces, wide_list).reshape(4, -1, 384)
        blocks = [
            near_shift(sent[0], -2),
            near_shift(sent[1], -1),
            near_shift(sent[2], 1),
            near_shift(sent[3], 2),
        ]
        received = jnp.concatenate(blocks, axis=0)
        bulk_rows = pick_rows(traces, bulk_list).reshape(2, -1, 384)
        below = bulk_shift(bulk_rows[1], 1)
        above = bulk_shift(bulk_rows[0], -1)
        table = jnp.concatenate([traces, received, below, above], axis=0)
        rows = jnp.take(table, source_rows, axis=0)
        turned = jnp.take_along_axis(rows, turn_index, axis=1)
        outside = jnp.where(boundary, traces * sign_cols[None, :], turned)
        jump = (
            (traces - outside).reshape(elems, 6, 6, 64).transpose(0, 2, 1, 3).reshape(elems, 6, 384)
        )
        d_e = (jump[:, 0], jump[:, 1], jump[:, 2])
        d_h = (jump[:, 3], jump[:, 4], jump[:, 5])
        cross_e = cross_with(normal, *d_e)
        cross_h = cross_with(normal, *d_h)
        e_inner = [z_out * d_h[comp] - cross_e[comp] for comp in range(3)]
        h_inner = [d_e[comp] / z_out + cross_h[comp] for comp in range(3)]
        flux_e = cross_with(normal, *e_inner)
        flux_h = cross_with(normal, *h_inner)
        face_terms = jnp.stack(
            [e_factor * entry for entry in flux_e] + [h_factor * entry for entry in flux_h], axis=1
        )
        lifted = jnp.dot(
            face_terms.reshape(elems * 6, 384),
            lift_table,
            precision=lax.Precision.HIGHEST,
            preferred_element_type=jnp.float32,
        ).reshape(elems, 6, 512)
        slopes = jnp.dot(
            state.reshape(elems * 6, 512),
            slopes_table,
            precision=lax.Precision.HIGHEST,
            preferred_element_type=jnp.float32,
        ).reshape(elems, 6, 3, 512)

        def slope(component, axis_id):
            return slopes[:, component, axis_id] * scales[:, axis_id][:, None]

        curl_h = (slope(5, 1) - slope(4, 2), slope(3, 2) - slope(5, 0), slope(4, 0) - slope(3, 1))
        curl_e = (slope(2, 1) - slope(1, 2), slope(0, 2) - slope(2, 0), slope(1, 0) - slope(0, 1))
        volume = jnp.stack(
            [entry / permit for entry in curl_h] + [-entry / permea for entry in curl_e], axis=1
        )
        return volume + lifted

    first = rate_of(fields)
    second = rate_of(fields + TIME_STEP * first)
    return fields + 0.5 * TIME_STEP * (first + second)


def solution(mesh):
    in_specs = (
        P(("wide", "bulk"), None, None),
        P(("wide", "bulk"), None),
        P(),
        P(("wide", "bulk")),
        P(("wide", "bulk"), None),
        P(("wide", "bulk"), None),
        P(("wide", "bulk"), None),
        P("wide", "bulk", None, None),
        P("wide", "bulk", None, None),
    )
    out_specs = P(("wide", "bulk"), None, None)
    return jax.shard_map(local, mesh=mesh, in_specs=in_specs, out_specs=out_specs, check_vma=False)
```

profile of v0, /device:TPU:0, one launch (start us, length us, event | category | flops | bytes accessed | tf_op | source)
XLA Modules:
  0.0 1245.4 jit_solution(79091517594790542)
XLA Ops:
  0.0 0.7 broadcast_compare_fusion.2
  0.7 0.7 broadcast_maximum_fusion.2
  1.6 0.7 broadcast_maximum_fusion.1
  2.3 0.7 pad_clamp_fusion
  3.0 1.5 copy.103
  4.6 3.9 gather_fusion.2
  8.5 0.3 copy.104
  9.0 0.6 gather_fusion.4
  9.7 2.5 collective-permute-start.5
  12.3 0.7 gather_fusion.3
  13.1 1.6 collective-permute-start.3
  14.7 1.5 collective-permute-start.2
  16.2 2.2 collective-permute-start
  19.0 0.6 broadcast_divide_fusion
  20.8 5.3 convolution_bitcast_fusion
  26.1 0.7 constant_dynamic-update-slice_fusion.5
  26.8 0.7 constant_dynamic-update-slice_fusion.4
  27.6 0.7 constant_dynamic-update-slice_fusion.3
  28.3 0.7 constant_dynamic-update-slice_fusion.2
  29.0 0.7 constant_dynamic-update-slice_fusion.1
  29.7 0.7 constant_dynamic-update-slice_fusion
  30.8 1.1 gather_fusion.1
  32.0 1.1 gather_fusion
  33.3 1.7 collective-permute-start.1
  35.0 2.4 collective-permute-done.1
  37.5 0.9 gather_fusion.5
  38.5 584.4 %gather_fusion.6 = f32[73728]{0:T(1024)S(1)} fusion(f32[192,384]{1,0:T(8,128)S(1)} %broadcast_select_fusion.1, s32[73728]{0:T(1024)S(1)} %reshape.2249), kind=kCustom, calls=%fused_computation.4.clone | custom fusion | bytes 1179648 | tf_op jit(solution)/shard_map/jit(take_along_axis)/gather | solution.py:176
  623.0 0.8 fusion.7
  624.4 0.7 constant_dynamic-update-slice_fusion.18
  625.1 0.8 constant_dynamic-update-slice_fusion.15
  626.0 2.6 multiply_add_fusion
  628.5 0.5 copy.118
  629.0 5.5 gather_fusion.7
  634.6 1.6 copy.114
  636.3 0.7 gather_fusion.9
  637.0 0.8 gather_fusion.8
  637.8 5.2 fusion.3
  643.9 0.5 copy-done.5
  644.4 1.8 collective-permute-start.6
  646.3 0.5 collective-permute-start.10
  646.8 0.2 collective-permute-start.9
  647.0 2.7 collective-permute-start.8
  649.7 4.5 collective-permute-start.7
  654.2 1.5 collective-permute-done.7
  655.8 1.0 gather_fusion.10
  656.9 584.4 %gather_fusion.11 = f32[73728]{0:T(1024)S(1)} fusion(f32[192,384]{1,0:T(8,128)S(1)} %broadcast_select_fusion, s32[73728]{0:T(1024)S(1)} %reshape.2249), kind=kCustom, calls=%fused_computation.9.clone | custom fusion | bytes 1179648 | tf_op jit(solution)/shard_map/jit(take_along_axis)/gather | solution.py:176
  1242.3 0.4 copy-done.3
  1242.8 2.6 fusion.2
  (195 shorter events, 5.6 us)
Async XLA Ops:
  1.5 8.1 copy-start.30
  1.6 8.1 copy-start.32
  3.0 5.9 copy-start.10
  4.5 7.7 copy-start.23
  4.5 14.0 %copy-start.43 = (f32[8,2]{0,1:T(2,128)S(1)}, f32[8,2]{0,1:T(2,128)}, u32[]{:S(2)}) copy-start(f32[8,2]{0,1:T(2,128)} %param.30) | copy-start | bytes 196
  4.5 14.0 %copy-start.19 = (s32[32,6]{0,1:T(8,128)S(1)}, s32[32,6]{0,1:T(8,128)}, u32[]{:S(2)}) copy-start(s32[32,6]{0,1:T(8,128)} %param.34) | copy-start | bytes 2308
  4.6 14.3 %copy-start.44 = (s32[32]{0:T(128)S(1)}, s32[32]{0:T(128)}, u32[]{:S(2)}) copy-start(s32[32]{0:T(128)} %param.31) | copy-start | bytes 388
  4.6 15.0 %copy-start = (f32[32,3]{0,1:T(4,128)S(1)}, f32[32,3]{0,1:T(4,128)}, u32[]{:S(2)}) copy-start(f32[32,3]{0,1:T(4,128)} %param.29) | copy-start | bytes 1156
  4.6 15.0 %copy-start.28 = (s32[32,6]{0,1:T(8,128)S(1)}, s32[32,6]{0,1:T(8,128)}, u32[]{:S(2)}) copy-start(s32[32,6]{0,1:T(8,128)} %param.33) | copy-start | bytes 2308
  4.6 15.2 %copy-start.29 = (s32[32,6]{0,1:T(8,128)S(1)}, s32[32,6]{0,1:T(8,128)}, u32[]{:S(2)}) copy-start(s32[32,6]{0,1:T(8,128)} %param.32) | copy-start | bytes 2308
  8.5 12.3 copy-start.1
  9.0 4.1 copy-start.24
  9.7 27.7 %collective-permute-start.5 = (f32[16,384]{1,0:T(8,128)S(1)}, f32[16,384]{1,0:T(8,128)S(1)}, u32[]{:S(2)}, u32[]{:S(2)}) collective-permute-start(f32[16,384]{1,0:T(8,128)S(1)} %get-tuple-element.47), channel_id=1, source_target_pairs={{0,3},{1,0},{2,1},{3,2},{4,7},{5,4},{6,5},{7,6},{8,11},{9,8},{10,9... | collective-permute-start | bytes 73736 | tf_op jit(solution)/shard_map/ppermute | solution.py:14
  12.2 25.2 %collective-permute-start.4 = (f32[16,384]{1,0:T(8,128)S(1)}, f32[16,384]{1,0:T(8,128)S(1)}, u32[]{:S(2)}, u32[]{:S(2)}) collective-permute-start(f32[16,384]{1,0:T(8,128)S(1)} %get-tuple-element.48), channel_id=1, source_target_pairs={{0,1},{1,2},{2,3},{3,0},{4,5},{5,6},{6,7},{7,4},{8,9},{9,10},{10,1... | collective-permute-start | bytes 73736 | tf_op jit(solution)/shard_map/ppermute | solution.py:14
  12.2 13.9 %copy-start.34 = (pred[64]{0:T(512)(128)(4,1)}, pred[64]{0:T(512)(128)(4,1)S(1)}, u32[]{:S(2)}) copy-start(pred[64]{0:T(512)(128)(4,1)S(1)} %compare_and_fusion.3) | copy-start | bytes 196
  12.3 6.2 copy-start.36
  13.1 24.3 %collective-permute-start.3 = (f32[16,384]{1,0:T(8,128)S(1)}, f32[16,384]{1,0:T(8,128)S(1)}, u32[]{:S(2)}, u32[]{:S(2)}) collective-permute-start(f32[16,384]{1,0:T(8,128)S(1)} %get-tuple-element.41), channel_id=1, source_target_pairs={{0,8},{4,12},{8,16},{12,20},{16,24},{20,28},{24,0},{28,4},{1,9},{5... | collective-permute-start | bytes 73736 | tf_op jit(solution)/shard_map/ppermute | solution.py:14
  14.7 22.6 %collective-permute-start.2 = (f32[16,384]{1,0:T(8,128)S(1)}, f32[16,384]{1,0:T(8,128)S(1)}, u32[]{:S(2)}, u32[]{:S(2)}) collective-permute-start(f32[16,384]{1,0:T(8,128)S(1)} %get-tuple-element.42), channel_id=1, source_target_pairs={{0,4},{4,8},{8,12},{12,16},{16,20},{20,24},{24,28},{28,0},{1,5},{5... | collective-permute-start | bytes 73736 | tf_op jit(solution)/shard_map/ppermute | solution.py:14
  16.2 17.1 %collective-permute-start = (f32[16,384]{1,0:T(8,128)S(1)}, f32[16,384]{1,0:T(8,128)S(1)}, u32[]{:S(2)}, u32[]{:S(2)}) collective-permute-start(f32[16,384]{1,0:T(8,128)S(1)} %get-tuple-element.44), channel_id=1, source_target_pairs={{0,24},{4,28},{8,0},{12,4},{16,8},{20,12},{24,16},{28,20},{1,25},{... | collective-permute-start | bytes 73736 | tf_op jit(solution)/shard_map/ppermute | solution.py:14
  18.8 19.6 %copy-start.41 = (pred[192]{0:T(512)(128)(4,1)}, pred[192]{0:T(512)(128)(4,1)S(1)}, u32[]{:S(2)}) copy-start(pred[192]{0:T(512)(128)(4,1)S(1)} %compare_and_fusion.1) | copy-start | bytes 580
  18.9 8.6 copy-start.17
  18.9 10.8 copy-start.15
  19.6 9.4 copy-start.13
  19.6 10.1 copy-start.11
  20.7 9.8 copy-start.38
  20.7 9.8 copy-start.39
  30.6 7.9 copy-start.20
  30.8 592.2 %copy-start.26 = (pred[192]{0:T(512)(128)(4,1)}, pred[192]{0:T(512)(128)(4,1)S(1)}, u32[]{:S(2)}) copy-start(pred[192]{0:T(512)(128)(4,1)S(1)} %lt.70) | copy-start | bytes 580
  33.3 4.1 collective-permute-start.1
  38.5 584.6 %copy-start.21 = (f32[384]{0:T(512)S(1)}, f32[384]{0:T(512)}, u32[]{:S(2)}) copy-start(f32[384]{0:T(512)} %constant.161.clone) | copy-start | bytes 4612
  636.2 6.8 copy-start.12
  636.2 6.8 copy-start.14
  636.3 6.8 copy-start.18
  637.0 6.4 copy-start.16
  637.8 5.9 copy-start.31
  637.8 5.9 copy-start.33
  637.8 6.0 copy-start.35
  637.8 6.0 copy-start.37
  643.1 13.7 %copy-start.42 = (pred[192]{0:T(512)(128)(4,1)S(1)}, pred[192]{0:T(512)(128)(4,1)}, u32[]{:S(2)}) copy-start(pred[192]{0:T(512)(128)(4,1)} %copy-done.41) | copy-start | bytes 580
  644.4 5.3 collective-permute-start.6
  646.3 9.5 collective-permute-start.11
  646.3 9.4 collective-permute-start.10
  646.8 8.9 collective-permute-start.9
  647.0 8.7 collective-permute-start.8
  649.7 6.0 collective-permute-start.7
  656.9 584.5 %copy-start.8 = (pred[192,384]{1,0:T(8,128)(4,1)S(1)}, pred[192,384]{1,0:T(8,128)(4,1)}, u32[]{:S(2)}) copy-start(pred[192,384]{1,0:T(8,128)(4,1)} %get-tuple-element.36) | copy-start | bytes 221188
  656.9 584.5 %copy-start.22 = (f32[384]{0:T(512)S(1)}, f32[384]{0:T(512)}, u32[]{:S(2)}) copy-start(f32[384]{0:T(512)} %constant.161.clone) | copy-start | bytes 4612
  656.9 584.5 %copy-start.27 = (pred[192]{0:T(512)(128)(4,1)S(1)}, pred[192]{0:T(512)(128)(4,1)}, u32[]{:S(2)}) copy-start(pred[192]{0:T(512)(128)(4,1)} %copy-done.26) | copy-start | bytes 580
  (9 other events, 14.3 us)
where the time goes:
time: 1250 us
  local copies, waits for them, and re-layouts  1190 us (95%)
  starting transfers between devices  19.2 us (2%)
  matrix products  15.6 us (1%)
    gather x5, local copies, waits for them, and re-layouts, rate_of(): turned = jnp.take_along_axis(rows, turn_index, axis=1)  1170 us
  transfers between devices with their start and end apart: 12, of which 2 were waited for; matrix products, arithmetic and copies ran while one was open for 1% of the time, Pallas kernels for 0%

commit v1 on v0

v1 whole, which is shorter than its diff:
```python
import functools

import jax
import jax.numpy as jnp
import numpy as np
from jax import lax
from jax.experimental import pallas as pl
from jax.experimental.pallas import tpu as pltpu
from jax.sharding import PartitionSpec as P

TIME_STEP = 0.005
LIFT_WEIGHT = 28.0
WIDE_OFFSETS = (-2, -1, 1, 2)
MESH = pl.DeviceIdType.MESH
F32 = jnp.float32
BF16 = jnp.bfloat16


def legendre_value(degree, point):
    previous = 1.0
    current = point
    for order in range(1, degree):
        following = ((2 * order + 1) * point * current - order * previous) / (order + 1)
        previous = current
        current = following
    return current


def gll_numpy():
    degree = 7
    points = [
        -1.0,
        -0.8717401485096066,
        -0.5917001814331423,
        -0.2092992179024789,
        0.2092992179024789,
        0.5917001814331423,
        0.8717401485096066,
        1.0,
    ]
    values = [legendre_value(degree, point) for point in points]
    matrix = np.zeros((degree + 1, degree + 1))
    for row_index in range(degree + 1):
        for col_index in range(degree + 1):
            if row_index != col_index:
                matrix[row_index, col_index] = values[row_index] / (
                    values[col_index] * (points[row_index] - points[col_index])
                )
    matrix[0, 0] = -degree * (degree + 1) / 4.0
    matrix[degree, degree] = degree * (degree + 1) / 4.0
    return matrix


def face_nodes():
    nodes = np.zeros((6, 64), dtype=np.int64)
    for face in range(6):
        axis_id = face // 2
        level = 7 * (face % 2)
        for place in range(64):
            outer = place // 8
            inner = place % 8
            if axis_id == 0:
                coords = (level, outer, inner)
            elif axis_id == 1:
                coords = (outer, level, inner)
            else:
                coords = (outer, inner, level)
            nodes[face, place] = 64 * coords[0] + 8 * coords[1] + coords[2]
    return nodes


def halves(matrix):
    high = np.asarray(matrix, dtype=np.float32).astype(jnp.bfloat16)
    low = (matrix - high.astype(np.float64)).astype(np.float32).astype(jnp.bfloat16)
    return high, low


def constants(elems):
    pick = np.zeros((512, 384), dtype=np.float32)
    pick[face_nodes().reshape(-1), np.arange(384)] = 1.0
    turned = gll_numpy().T
    eye = np.eye(8)
    first = np.kron(turned, np.eye(64))
    second = np.kron(np.eye(2), np.kron(turned, eye))
    third = np.kron(np.eye(16), turned)
    d0 = np.stack(halves(first))
    d12 = np.concatenate([second, third], axis=1)
    high, low = halves(d12)
    d12 = np.concatenate([high, high, low], axis=0)
    turn = np.zeros((128, 8, 128), dtype=np.float32)
    for flag in range(8):
        for place in range(64):
            outer, inner = place // 8, place % 8
            outer = 7 - outer if flag & 1 else outer
            inner = 7 - inner if flag & 2 else inner
            source = inner * 8 + outer if flag & 4 else outer * 8 + inner
            for half in range(2):
                turn[half * 64 + source, flag, half * 64 + place] = 1.0
    turn = turn.reshape(128, 1024)
    turn = np.concatenate([turn, turn], axis=0)
    code = np.zeros((1, 6 * elems), dtype=np.float32)
    for face in range(6):
        code[0, face * elems : (face + 1) * elems] = 6 * np.arange(elems) + face
    return (
        jnp.asarray(pick, dtype=BF16),
        jnp.asarray(pick.T, dtype=BF16),
        jnp.asarray(d0),
        jnp.asarray(d12),
        jnp.asarray(turn, dtype=BF16),
        jnp.asarray(code),
    )


def split(value):
    high = value.astype(BF16)
    low = (value - high.astype(F32)).astype(BF16)
    return high, low


def mul(left, right):
    return jnp.dot(left, right, preferred_element_type=F32)


def column(row):
    size = row.shape[1]
    shape = (size, size)
    same = lax.broadcasted_iota(jnp.int32, shape, 0) == lax.broadcasted_iota(jnp.int32, shape, 1)
    return jnp.sum(jnp.where(same, jnp.broadcast_to(row, shape), 0.0), axis=1, keepdims=True)


def swap(value):
    return pltpu.roll(value, 64, 1)


def kernel(
    fields_ref,
    scales_ref,
    class_ref,
    material_ref,
    neighbour_ref,
    orient_ref,
    source_ref,
    wide_ref,
    bulk_ref,
    pick_ref,
    lift_ref,
    d0_ref,
    d12_ref,
    turn_ref,
    code_ref,
    out_ref,
    state_ref,
    rate_ref,
    table_ref,
    own_ref,
    far_ref,
    choose_ref,
    coef_ref,
    send_ref,
    recv_ref,
    send_sem,
    recv_sem,
):
    elems = fields_ref.shape[0]
    faces = 6 * elems
    slot = wide_ref.shape[3]
    wide_id, bulk_id = lax.axis_index("wide"), lax.axis_index("bulk")
    n_wide, n_bulk = lax.axis_size("wide"), lax.axis_size("bulk")
    targets = [(lax.rem(wide_id + offset + n_wide, n_wide), bulk_id) for offset in WIDE_OFFSETS]
    targets.append((wide_id, lax.rem(bulk_id + 1, n_bulk)))
    targets.append((wide_id, lax.rem(bulk_id + n_bulk - 1, n_bulk)))

    barrier = pltpu.get_barrier_semaphore()
    for target in targets:
        pl.semaphore_signal(barrier, inc=1, device_id=target, device_id_type=MESH)

    for comp in range(6):
        state_ref[comp * elems : (comp + 1) * elems, :] = fields_ref[:, comp, :]

    code = code_ref[...]
    wide_rows = wide_ref[0, 0].astype(F32)
    bulk_rows = bulk_ref[0, 0].astype(F32)
    order = [wide_rows[q : q + 1] for q in range(4)] + [bulk_rows[1:2], bulk_rows[0:1]]
    for q, row in enumerate(order):
        choose_ref[q * slot : (q + 1) * slot, :] = jnp.where(column(row) == code, 1.0, 0.0).astype(BF16)

    low_half = lax.broadcasted_iota(jnp.int32, (elems, 128), 1) < 64
    source = source_ref[...].astype(F32)
    far_code = (lax.broadcasted_iota(jnp.int32, (elems, 6 * slot), 1) + faces).astype(F32)
    material = column(material_ref[...].astype(F32))
    neighbour = neighbour_ref[...]
    table = class_ref[...]
    imped = jnp.sqrt(table[:, 1:2] / table[:, 0:1])
    permit = jnp.zeros((elems, 1), F32)
    permea = jnp.zeros((elems, 1), F32)
    own_imp = jnp.zeros((elems, 1), F32)
    z_all = jnp.zeros((elems, 6), F32)
    for entry in range(class_ref.shape[0]):
        hit = material == float(entry)
        permit = permit + jnp.where(hit, table[entry : entry + 1, 0:1], 0.0)
        permea = permea + jnp.where(hit, table[entry : entry + 1, 1:2], 0.0)
        own_imp = own_imp + jnp.where(hit, imped[entry : entry + 1, :], 0.0)
        z_all = z_all + jnp.where(neighbour == entry, imped[entry : entry + 1, :], 0.0)
    inv_eps = 1.0 / permit
    inv_mu = 1.0 / permea
    scale = [scales_ref[:, axis : axis + 1] for axis in range(3)]
    for face in range(6):
        rows = slice(face * elems, (face + 1) * elems)
        sign = 2.0 * (face % 2) - 1.0
        origin = source[:, face : face + 1]
        own_ref[rows, :] = jnp.where(origin == code, 1.0, 0.0).astype(BF16)
        far_ref[rows, :] = jnp.where(origin == far_code, 1.0, 0.0).astype(BF16)
        z_out = z_all[:, face : face + 1]
        lift = LIFT_WEIGHT * scale[face // 2]
        e_factor = -lift / (permit * (own_imp + z_out))
        h_factor = lift / (permea * (1.0 / own_imp + 1.0 / z_out))
        coef_ref[0, rows, :] = jnp.where(low_half, e_factor, -h_factor)
        coef_ref[1, rows, :] = jnp.where(low_half, -sign * z_out * e_factor, -sign * h_factor / z_out)
        coef_ref[2, rows, :] = jnp.where(origin < 0.0, jnp.where(low_half, 2.0, 0.0), 1.0)
    orient = orient_ref[...]

    pl.semaphore_wait(barrier, len(targets))

    def stage(number):
        state = state_ref[...]
        high, low = split(state)
        pick = pick_ref[...]
        traces = mul(high, pick) + mul(low, pick)
        half = lax.broadcasted_iota(jnp.int32, (3 * elems, 128), 1) < 64
        for axis in range(3):
            e_part = traces[0 : 3 * elems, axis * 128 : (axis + 1) * 128]
            h_part = traces[3 * elems :, axis * 128 : (axis + 1) * 128]
            near = jnp.where(half, e_part, swap(h_part))
            away = jnp.where(half, swap(e_part), h_part)
            for side, part in enumerate((near, away)):
                first = (2 * axis + side) * elems
                for dim in range(3):
                    table_ref[first : first + elems, dim * 128 : (dim + 1) * 128] = part[
                        dim * elems : (dim + 1) * elems
                    ]
        tab_high, tab_low = split(table_ref[...])
        choose = choose_ref[...]
        sent = mul(choose, tab_high) + mul(choose, tab_low)
        copies = []
        for q, target in enumerate(targets):
            send_ref[number, q] = sent[q * slot : (q + 1) * slot]
        for q, target in enumerate(targets):
            copy = pltpu.make_async_remote_copy(
                src_ref=send_ref.at[number, q],
                dst_ref=recv_ref.at[number, q],
                send_sem=send_sem.at[number, q],
                recv_sem=recv_sem.at[number, q],
                device_id=target,
                device_id_type=MESH,
            )
            copy.start()
            copies.append(copy)

        slope0 = mul(high, d0_ref[0]) + mul(low, d0_ref[0]) + mul(high, d0_ref[1])
        wide_in = jnp.concatenate(
            [
                jnp.concatenate([part[:, block * 128 : (block + 1) * 128] for block in range(4)], axis=0)
                for part in (high, low, high)
            ],
            axis=1,
        )
        slope12 = mul(wide_in, d12_ref[...])

        def slope(comp, axis):
            if axis == 0:
                return slope0[comp * elems : (comp + 1) * elems]
            lanes = slice((axis - 1) * 128, axis * 128)
            return jnp.concatenate(
                [
                    slope12[(block * 6 + comp) * elems : (block * 6 + comp + 1) * elems, lanes]
                    for block in range(4)
                ],
                axis=1,
            )

        volume = []
        for field in range(2):
            other = 3 * (1 - field)
            factor = inv_eps if field == 0 else -inv_mu
            for dim in range(3):
                one, two = (dim + 1) % 3, (dim + 2) % 3
                volume.append(
                    (factor * scale[one]) * slope(other + two, one)
                    - (factor * scale[two]) * slope(other + one, two)
                )
        volume = jnp.concatenate(volume, axis=0)

        own = own_ref[...]
        got_high = mul(own, tab_high)
        got_low = mul(own, tab_low)
        for copy in copies:
            copy.wait()
        far_high, far_low = split(recv_ref[number].reshape(6 * slot, 384))
        far = far_ref[...]
        got_high = (got_high + mul(far, far_high)).astype(BF16)
        got_low = (got_low + mul(far, far_low)).astype(BF16)

        pieces = []
        for face in range(6):
            rows = slice(face * elems, (face + 1) * elems)
            for step in (1, 2):
                dim = (face // 2 + step) % 3
                lanes = slice(dim * 128, (dim + 1) * 128)
                pieces.append(jnp.concatenate([got_high[rows, lanes], got_low[rows, lanes]], axis=1))
        turned = mul(jnp.concatenate(pieces, axis=0), turn_ref[...])

        faces_out = {}
        for face in range(6):
            axis = face // 2
            rows = slice(face * elems, (face + 1) * elems)
            flag = jnp.broadcast_to(orient[:, face : face + 1], (elems, 128))
            jumps = []
            for step in (1, 2):
                dim = (axis + step) % 3
                first = (2 * face + step - 1) * elems
                forms = [turned[first : first + elems, o * 128 : (o + 1) * 128] for o in range(8)]
                for bit in (1, 2, 4):
                    chosen = (flag & bit) > 0
                    forms = [
                        jnp.where(chosen, forms[2 * o + 1], forms[2 * o]) for o in range(len(forms) // 2)
                    ]
                own_trace = table_ref[rows, dim * 128 : (dim + 1) * 128]
                jumps.append(own_trace * coef_ref[2, rows, :] - forms[0])
            straight = coef_ref[0, rows, :]
            crossed = coef_ref[1, rows, :]
            faces_out[face, (axis + 1) % 3] = straight * jumps[0] + crossed * swap(jumps[1])
            faces_out[face, (axis + 2) % 3] = straight * jumps[1] - crossed * swap(jumps[0])

        blank = jnp.zeros((elems, 128), F32)
        lines = []
        for field in range(2):
            for dim in range(3):
                line = []
                for axis in range(3):
                    if axis == dim:
                        line.append(blank)
                        continue
                    near, away = faces_out[2 * axis, dim], faces_out[2 * axis + 1, dim]
                    if field == 0:
                        line.append(jnp.where(low_half, near, swap(away)))
                    else:
                        line.append(jnp.where(low_half, swap(near), away))
                lines.append(jnp.concatenate(line, axis=1))
        lift_high, lift_low = split(jnp.concatenate(lines, axis=0))
        lift = lift_ref[...]
        return volume + mul(lift_high, lift) + mul(lift_low, lift)

    first = stage(0)
    rate_ref[...] = first
    state_ref[...] = state_ref[...] + TIME_STEP * first
    second = stage(1)
    total = rate_ref[...] + second
    for comp in range(6):
        rows = slice(comp * elems, (comp + 1) * elems)
        out_ref[:, comp, :] = fields_ref[:, comp, :] + 0.5 * TIME_STEP * total[rows]


def local(
    fields,
    scales,
    class_table,
    material,
    neighbour_class,
    orientation,
    face_source,
    wide_send,
    bulk_send,
):
    elems = fields.shape[0]
    slot = wide_send.shape[3]
    faces = 6 * elems
    vmem = pl.BlockSpec(memory_space=pltpu.VMEM)
    return pl.pallas_call(
        kernel,
        out_shape=jax.ShapeDtypeStruct(fields.shape, fields.dtype),
        in_specs=[vmem] * 15,
        out_specs=vmem,
        scratch_shapes=[
            pltpu.VMEM((faces, 512), F32),
            pltpu.VMEM((faces, 512), F32),
            pltpu.VMEM((faces, 384), F32),
            pltpu.VMEM((faces, faces), BF16),
            pltpu.VMEM((faces, 6 * slot), BF16),
            pltpu.VMEM((6 * slot, faces), BF16),
            pltpu.VMEM((3, faces, 128), F32),
            pltpu.VMEM((2, 6, slot, 384), F32),
            pltpu.VMEM((2, 6, slot, 384), F32),
            pltpu.SemaphoreType.DMA((2, 6)),
            pltpu.SemaphoreType.DMA((2, 6)),
        ],
        compiler_params=pltpu.CompilerParams(
            collective_id=0, has_side_effects=True, vmem_limit_bytes=48 * 1024 * 1024
        ),
    )(
        fields,
        scales,
        class_table,
        material.reshape(1, elems),
        neighbour_class,
        orientation,
        face_source,
        wide_send,
        bulk_send,
        *constants(elems),
    )


def solution(mesh):
    in_specs = (
        P(("wide", "bulk"), None, None),
        P(("wide", "bulk"), None),
        P(),
        P(("wide", "bulk")),
        P(("wide", "bulk"), None),
        P(("wide", "bulk"), None),
        P(("wide", "bulk"), None),
        P("wide", "bulk", None, None),
        P("wide", "bulk", None, None),
    )
    out_specs = P(("wide", "bulk"), None, None)
    return jax.shard_map(local, mesh=mesh, in_specs=in_specs, out_specs=out_specs, check_vma=False)
```

time: 1250 us -> 28.9 us (0.02)
  local copies, waits for them, and re-layouts: 1190 us -> 9.3 us
  starting transfers between devices: 19.2 us -> 0 us
  Pallas kernels: 0 us -> 19.1 us
  matrix products: 15.6 us -> 0 us
    gather x19 -> x0, local copies, waits for them, and re-layouts: 1190 us -> none  [the longest x5 1170 us: rate_of(): turned = jnp.take_along_axis(rows, turn_index, axis=1)]
    ppermute x12 -> x0, starting transfers between devices: 19.2 us -> none  [from_behind(): return lax.ppermute(value, axis, pairs)]
    pallas_call x0 -> x1, Pallas kernels: none -> 19.1 us  [local(): pl.pallas_call(kernel, out_shape=jax.ShapeDtypeStruct(fields.shape, field...]
    dot_general x4 -> x0, matrix products: 15.6 us -> none  [the longest x2 10.5 us: rate_of(): jnp.dot(state.reshape(elems * 6, 512), slopes_table, precision=lax.Precis...]
  transfers between devices with their start and end apart: 12 -> 0, of which waited for: 2 -> 0; matrix products, arithmetic and copies ran while one was open for 1% -> 0% of each run, Pallas kernels for 0% -> 0%
where the time goes in v1:
time: 28.9 us; the launch traced here: 28.5 us
  Pallas kernels  19.1 us (66%)
  local copies, waits for them, and re-layouts  9.3 us (32%)
    pallas_call x1, Pallas kernels, local(): pl.pallas_call(kernel, out_shape=jax.ShapeDtypeStruct(fields.shape, field...  19.1 us
    unnamed x24, local copies, waits for them, and re-layouts  8.33 us
    pallas_call x1, local copies, waits for them, and re-layouts, local(): pl.pallas_call(kernel, out_shape=jax.ShapeDtypeStruct(fields.shape, field...  0.98 us

profile of v1, /device:TPU:0, one launch (start us, length us, event | category | flops | bytes accessed | tf_op | source)
XLA Modules:
  0.0 28.5 jit_solution(9042608100210352785)
XLA Ops:
  0.0 0.0 copy-start.1
  0.0 0.8 %copy.18.class_ref = f32[8,2]{1,0:T(8,128)S(1)} copy(f32[8,2]{0,1:T(2,128)} %param.17) | data formatting | bytes 128 | tf_op args[2]
  0.8 0.8 %copy.17.scales_ref = f32[32,3]{1,0:T(8,128)S(1)} copy(f32[32,3]{0,1:T(4,128)} %param.16) | data formatting | bytes 768 | tf_op args[1]
  1.6 0.8 %copy.19.neighbour_ref = s32[32,6]{1,0:T(8,128)S(1)} copy(s32[32,6]{0,1:T(8,128)} %param.19) | data formatting | bytes 1536 | tf_op args[4]
  2.3 0.8 %copy.20.orient_ref = s32[32,6]{1,0:T(8,128)S(1)} copy(s32[32,6]{0,1:T(8,128)} %param.20) | data formatting | bytes 1536 | tf_op args[5]
  3.1 0.8 %copy.21.source_ref = s32[32,6]{1,0:T(8,128)S(1)} copy(s32[32,6]{0,1:T(8,128)} %param.21) | data formatting | bytes 1536 | tf_op args[6]
  3.9 0.0 copy-start.2
  3.9 0.0 copy-start.5
  3.9 0.0 copy-start.6
  3.9 0.0 copy-start.7
  3.9 0.0 copy-start.8
  3.9 1.3 %copy.16.fields_ref = f32[32,6,512]{2,1,0:T(8,128)S(1)} copy(f32[32,6,512]{2,0,1:T(8,128)} %param.15) | data formatting | bytes 786432 | tf_op args[0]
  5.2 0.0 copy-done.1
  5.2 0.0 copy-done.2
  5.2 0.0 copy-done.5
  5.2 0.0 copy-done.6
  5.2 0.0 copy-done.7
  5.2 0.0 copy-done.8
  5.3 0.0 copy-start
  5.3 1.2 %copy-done = bf16[2,512,512]{2,1,0:T(8,128)(2,1)S(1)} copy-done((bf16[2,512,512]{2,1,0:T(8,128)(2,1)S(1)}, bf16[2,512,512]{2,1,0:T(8,128)(2,1)}, u32[]{:S(2)}) %copy-start) | copy-done | bytes 1048600
  6.5 0.0 copy-start.3
  6.5 1.0 %copy-done.3 = bf16[512,384]{1,0:T(8,128)(2,1)S(1)} copy-done((bf16[512,384]{1,0:T(8,128)(2,1)S(1)}, bf16[512,384]{1,0:T(8,128)(2,1)}, u32[]{:S(2)}) %copy-start.3) | copy-done | bytes 393240
  7.5 0.0 copy-start.4
  7.5 0.9 %copy-done.4 = bf16[384,256]{1,0:T(8,128)(2,1)S(1)} copy-done((bf16[384,256]{1,0:T(8,128)(2,1)S(1)}, bf16[384,256]{1,0:T(8,128)(2,1)}, u32[]{:S(2)}) %copy-start.4) | copy-done | bytes 196632
  8.4 19.1 %shard_map.145 = f32[32,6,512]{2,1,0:T(8,128)S(1)} custom-call(f32[32,6,512]{2,1,0:T(8,128)S(1)} %copy.16.fields_ref, f32[32,3]{1,0:T(8,128)S(1)} %copy.17.scales_ref, f32[8,2]{1,0:T(8,128)S(1)} %copy.18.class_ref, s32[1,32]{1,0:T(1,128)S(1)} %bitcast.1, s32[32,6]{1,0:T(8,128)S(1)} %copy.19.neighbour_ref, s32[32,6]{1,0:T(8,128)S(1)} %copy.20.orient_ref, ...), custom_call_target="tpu_custom_call" | custom-call | tf_op jit(solution)/shard_map/pallas_call | solution.py:378
  27.5 1.0 %copy.22 = f32[32,6,512]{2,0,1:T(8,128)} copy(f32[32,6,512]{2,1,0:T(8,128)S(1)} %shard_map.145) | data formatting | bytes 786432 | tf_op jit(solution)/shard_map/pallas_call | solution.py:378
Async XLA Ops:
  0.0 5.2 %copy-start.1 = (bf16[256,1024]{1,0:T(8,128)(2,1)S(1)}, bf16[256,1024]{1,0:T(8,128)(2,1)}, u32[]{:S(2)}) copy-start(bf16[256,1024]{1,0:T(8,128)(2,1)} %constant.16.clone.turn_ref) | copy-start | bytes 1572868
  3.9 1.3 %copy-start.2 = (bf16[384,512]{1,0:T(8,128)(2,1)S(1)}, bf16[384,512]{1,0:T(8,128)(2,1)}, u32[]{:S(2)}) copy-start(bf16[384,512]{1,0:T(8,128)(2,1)} %constant.13.clone.lift_ref) | copy-start | bytes 1179652
  3.9 1.3 %copy-start.5 = (s32[1,1,4,16]{3,2,1,0:T(4,128)S(1)}, s32[1,1,4,16]{3,2,1,0:T(4,128)}, u32[]{:S(2)}) copy-start(s32[1,1,4,16]{3,2,1,0:T(4,128)} %wide_ref.1) | copy-start | bytes 772
  3.9 1.3 %copy-start.6 = (s32[1,1,2,16]{3,2,1,0:T(2,128)S(1)}, s32[1,1,2,16]{3,2,1,0:T(2,128)}, u32[]{:S(2)}) copy-start(s32[1,1,2,16]{3,2,1,0:T(2,128)} %bulk_ref.1) | copy-start | bytes 388
  3.9 1.4 %copy-start.7 = (f32[1,192]{1,0:T(1,128)S(1)}, f32[1,192]{1,0:T(1,128)}, u32[]{:S(2)}) copy-start(f32[1,192]{1,0:T(1,128)} %constant.17.clone.code_ref) | copy-start | bytes 2308
  3.9 1.3 %copy-start.8 = (s32[32]{0:T(128)S(1)}, s32[32]{0:T(128)}, u32[]{:S(2)}) copy-start(s32[32]{0:T(128)} %param.18) | copy-start | bytes 388
  5.3 1.2 %copy-start = (bf16[2,512,512]{2,1,0:T(8,128)(2,1)S(1)}, bf16[2,512,512]{2,1,0:T(8,128)(2,1)}, u32[]{:S(2)}) copy-start(bf16[2,512,512]{2,1,0:T(8,128)(2,1)} %constant.14.clone.d0_ref) | copy-start | bytes 3145732
  6.5 1.0 %copy-start.3 = (bf16[512,384]{1,0:T(8,128)(2,1)S(1)}, bf16[512,384]{1,0:T(8,128)(2,1)}, u32[]{:S(2)}) copy-start(bf16[512,384]{1,0:T(8,128)(2,1)} %constant.12.clone.pick_ref) | copy-start | bytes 1179652
  7.5 0.9 %copy-start.4 = (bf16[384,256]{1,0:T(8,128)(2,1)S(1)}, bf16[384,256]{1,0:T(8,128)(2,1)}, u32[]{:S(2)}) copy-start(bf16[384,256]{1,0:T(8,128)(2,1)} %constant.15.clone.d12_ref) | copy-start | bytes 589828

commit v2 on v1

--- a/solution.py
+++ b/solution.py
@@ -133,7 +133,7 @@
 
 
 def kernel(
-    fields_ref,
+    fields_hbm,
     scales_ref,
     class_ref,
     material_ref,
@@ -142,15 +142,21 @@
     source_ref,
     wide_ref,
     bulk_ref,
+    pick_hbm,
+    lift_hbm,
+    d0_hbm,
+    d12_hbm,
+    turn_hbm,
+    code_ref,
+    out_ref,
+    state_ref,
+    base_ref,
     pick_ref,
     lift_ref,
     d0_ref,
     d12_ref,
     turn_ref,
-    code_ref,
-    out_ref,
-    state_ref,
-    rate_ref,
+    small_ref,
     table_ref,
     own_ref,
     far_ref,
@@ -158,10 +164,11 @@
     coef_ref,
     send_ref,
     recv_ref,
+    load_sem,
     send_sem,
     recv_sem,
 ):
-    elems = fields_ref.shape[0]
+    elems = material_ref.shape[1]
     faces = 6 * elems
     slot = wide_ref.shape[3]
     wide_id, bulk_id = lax.axis_index("wide"), lax.axis_index("bulk")
@@ -174,8 +181,20 @@
     for target in targets:
         pl.semaphore_signal(barrier, inc=1, device_id=target, device_id_type=MESH)
 
-    for comp in range(6):
-        state_ref[comp * elems : (comp + 1) * elems, :] = fields_ref[:, comp, :]
+    loads = []
+    for place, (source, target) in enumerate(
+        (
+            (fields_hbm, state_ref),
+            (pick_hbm, pick_ref),
+            (d0_hbm, d0_ref),
+            (d12_hbm, d12_ref),
+            (turn_hbm, turn_ref),
+            (lift_hbm, lift_ref),
+        )
+    ):
+        load = pltpu.make_async_copy(source, target, load_sem.at[place])
+        load.start()
+        loads.append(load)
 
     code = code_ref[...]
     wide_rows = wide_ref[0, 0].astype(F32)
@@ -185,47 +204,61 @@
         choose_ref[q * slot : (q + 1) * slot, :] = jnp.where(column(row) == code, 1.0, 0.0).astype(BF16)
 
     low_half = lax.broadcasted_iota(jnp.int32, (elems, 128), 1) < 64
-    source = source_ref[...].astype(F32)
     far_code = (lax.broadcasted_iota(jnp.int32, (elems, 6 * slot), 1) + faces).astype(F32)
-    material = column(material_ref[...].astype(F32))
+    material = material_ref[...]
     neighbour = neighbour_ref[...]
     table = class_ref[...]
-    imped = jnp.sqrt(table[:, 1:2] / table[:, 0:1])
-    permit = jnp.zeros((elems, 1), F32)
-    permea = jnp.zeros((elems, 1), F32)
-    own_imp = jnp.zeros((elems, 1), F32)
-    z_all = jnp.zeros((elems, 6), F32)
-    for entry in range(class_ref.shape[0]):
-        hit = material == float(entry)
-        permit = permit + jnp.where(hit, table[entry : entry + 1, 0:1], 0.0)
-        permea = permea + jnp.where(hit, table[entry : entry + 1, 1:2], 0.0)
-        own_imp = own_imp + jnp.where(hit, imped[entry : entry + 1, :], 0.0)
-        z_all = z_all + jnp.where(neighbour == entry, imped[entry : entry + 1, :], 0.0)
-    inv_eps = 1.0 / permit
-    inv_mu = 1.0 / permea
-    scale = [scales_ref[:, axis : axis + 1] for axis in range(3)]
+    imped = jnp.sqrt(table[1:2, :] / table[0:1, :])
+    permit = jnp.zeros((1, elems), F32)
+    permea = jnp.zeros((1, elems), F32)
+    own_imp = jnp.zeros((1, elems), F32)
+    z_out = jnp.zeros((6, elems), F32)
+    for entry in range(class_ref.shape[1]):
+        hit = material == entry
+        permit = permit + jnp.where(hit, table[0:1, entry : entry + 1], 0.0)
+        permea = permea + jnp.where(hit, table[1:2, entry : entry + 1], 0.0)
+        own_imp = own_imp + jnp.where(hit, imped[:, entry : entry + 1], 0.0)
+        z_out = z_out + jnp.where(neighbour == entry, imped[:, entry : entry + 1], 0.0)
+    side = lax.broadcasted_iota(jnp.int32, (6, elems), 0)
+    sign = jnp.where((side & 1) > 0, 1.0, -1.0)
+    scales = scales_ref[...]
+    lift = LIFT_WEIGHT * jnp.where(side < 2, scales[0:1], jnp.where(side < 4, scales[1:2], scales[2:3]))
+    e_factor = -lift / (permit * (own_imp + z_out))
+    h_factor = lift / (permea * (1.0 / own_imp + 1.0 / z_out))
+    small_ref[...] = jnp.zeros_like(small_ref)
+    small_ref[0:6, 0:elems] = source_ref[...].astype(F32)
+    small_ref[8:14, 0:elems] = orient_ref[...].astype(F32)
+    small_ref[16:22, 0:elems] = e_factor
+    small_ref[24:30, 0:elems] = -h_factor
+    small_ref[32:38, 0:elems] = -sign * z_out * e_factor
+    small_ref[40:46, 0:elems] = -sign * h_factor / z_out
+    small_ref[48:51, 0:elems] = scales / permit
+    small_ref[56:59, 0:elems] = -scales / permea
+    columns = jnp.transpose(small_ref[...])[0:elems]
+
+    def col(group, index):
+        return columns[:, 8 * group + index : 8 * group + index + 1]
+
+    flags = []
     for face in range(6):
         rows = slice(face * elems, (face + 1) * elems)
-        sign = 2.0 * (face % 2) - 1.0
-        origin = source[:, face : face + 1]
+        origin = col(0, face)
         own_ref[rows, :] = jnp.where(origin == code, 1.0, 0.0).astype(BF16)
         far_ref[rows, :] = jnp.where(origin == far_code, 1.0, 0.0).astype(BF16)
-        z_out = z_all[:, face : face + 1]
-        lift = LIFT_WEIGHT * scale[face // 2]
-        e_factor = -lift / (permit * (own_imp + z_out))
-        h_factor = lift / (permea * (1.0 / own_imp + 1.0 / z_out))
-        coef_ref[0, rows, :] = jnp.where(low_half, e_factor, -h_factor)
-        coef_ref[1, rows, :] = jnp.where(low_half, -sign * z_out * e_factor, -sign * h_factor / z_out)
+        coef_ref[0, rows, :] = jnp.where(low_half, col(2, face), col(3, face))
+        coef_ref[1, rows, :] = jnp.where(low_half, col(4, face), col(5, face))
         coef_ref[2, rows, :] = jnp.where(origin < 0.0, jnp.where(low_half, 2.0, 0.0), 1.0)
-    orient = orient_ref[...]
+        coef_ref[3, rows, :] = jnp.broadcast_to(col(1, face), (elems, 128))
 
     pl.semaphore_wait(barrier, len(targets))
 
     def stage(number):
-        state = state_ref[...]
-        high, low = split(state)
-        pick = pick_ref[...]
-        traces = mul(high, pick) + mul(low, pick)
+        if number == 0:
+            loads[0].wait()
+            loads[1].wait()
+        high, low = split(state_ref[...])
+        both = mul(jnp.concatenate([high, low], axis=0), pick_ref[...])
+        traces = both[0:faces] + both[faces:]
         half = lax.broadcasted_iota(jnp.int32, (3 * elems, 128), 1) < 64
         for axis in range(3):
             e_part = traces[0 : 3 * elems, axis * 128 : (axis + 1) * 128]
@@ -238,9 +271,9 @@
                     table_ref[first : first + elems, dim * 128 : (dim + 1) * 128] = part[
                         dim * elems : (dim + 1) * elems
                     ]
-        tab_high, tab_low = split(table_ref[...])
-        choose = choose_ref[...]
-        sent = mul(choose, tab_high) + mul(choose, tab_low)
+        tab = jnp.concatenate(split(table_ref[...]), axis=1)
+        sent = mul(choose_ref[...], tab)
+        sent = sent[:, 0:384] + sent[:, 384:]
         copies = []
         for q, target in enumerate(targets):
             send_ref[number, q] = sent[q * slot : (q + 1) * slot]
@@ -256,7 +289,13 @@
             copy.start()
             copies.append(copy)
 
-        slope0 = mul(high, d0_ref[0]) + mul(low, d0_ref[0]) + mul(high, d0_ref[1])
+        if number == 0:
+            loads[2].wait()
+            loads[3].wait()
+        active = jnp.concatenate([high[elems : 3 * elems], high[4 * elems :]], axis=0)
+        active_low = jnp.concatenate([low[elems : 3 * elems], low[4 * elems :]], axis=0)
+        slope0 = mul(jnp.concatenate([active, active_low], axis=0), d0_ref[0])
+        slope0 = slope0[0 : 4 * elems] + slope0[4 * elems :] + mul(active, d0_ref[1])
         wide_in = jnp.concatenate(
             [
                 jnp.concatenate([part[:, block * 128 : (block + 1) * 128] for block in range(4)], axis=0)
@@ -268,7 +307,8 @@
 
         def slope(comp, axis):
             if axis == 0:
-                return slope0[comp * elems : (comp + 1) * elems]
+                place = 2 * (comp // 3) + comp % 3 - 1
+                return slope0[place * elems : (place + 1) * elems]
             lanes = slice((axis - 1) * 128, axis * 128)
             return jnp.concatenate(
                 [
@@ -281,39 +321,44 @@
         volume = []
         for field in range(2):
             other = 3 * (1 - field)
-            factor = inv_eps if field == 0 else -inv_mu
             for dim in range(3):
                 one, two = (dim + 1) % 3, (dim + 2) % 3
                 volume.append(
-                    (factor * scale[one]) * slope(other + two, one)
-                    - (factor * scale[two]) * slope(other + one, two)
+                    col(6 + field, one) * slope(other + two, one)
+                    - col(6 + field, two) * slope(other + one, two)
                 )
         volume = jnp.concatenate(volume, axis=0)
 
-        own = own_ref[...]
-        got_high = mul(own, tab_high)
-        got_low = mul(own, tab_low)
+        got = mul(own_ref[...], tab)
+        if number == 0:
+            loads[4].wait()
+            loads[5].wait()
         for copy in copies:
             copy.wait()
-        far_high, far_low = split(recv_ref[number].reshape(6 * slot, 384))
-        far = far_ref[...]
-        got_high = (got_high + mul(far, far_high)).astype(BF16)
-        got_low = (got_low + mul(far, far_low)).astype(BF16)
+        beyond = jnp.concatenate(split(recv_ref[number].reshape(6 * slot, 384)), axis=1)
+        got = (got + mul(far_ref[...], beyond)).astype(BF16)
 
         pieces = []
         for face in range(6):
             rows = slice(face * elems, (face + 1) * elems)
             for step in (1, 2):
                 dim = (face // 2 + step) % 3
-                lanes = slice(dim * 128, (dim + 1) * 128)
-                pieces.append(jnp.concatenate([got_high[rows, lanes], got_low[rows, lanes]], axis=1))
+                pieces.append(
+                    jnp.concatenate(
+                        [
+                            got[rows, dim * 128 : (dim + 1) * 128],
+                            got[rows, 384 + dim * 128 : 384 + (dim + 1) * 128],
+                        ],
+                        axis=1,
+                    )
+                )
         turned = mul(jnp.concatenate(pieces, axis=0), turn_ref[...])
 
         faces_out = {}
         for face in range(6):
             axis = face // 2
             rows = slice(face * elems, (face + 1) * elems)
-            flag = jnp.broadcast_to(orient[:, face : face + 1], (elems, 128))
+            flag = coef_ref[3, rows, :].astype(jnp.int32)
             jumps = []
             for step in (1, 2):
                 dim = (axis + step) % 3
@@ -346,18 +391,15 @@
                     else:
                         line.append(jnp.where(low_half, swap(near), away))
                 lines.append(jnp.concatenate(line, axis=1))
-        lift_high, lift_low = split(jnp.concatenate(lines, axis=0))
-        lift = lift_ref[...]
-        return volume + mul(lift_high, lift) + mul(lift_low, lift)
+        lifted = mul(jnp.concatenate(split(jnp.concatenate(lines, axis=0)), axis=0), lift_ref[...])
+        return volume + (lifted[0:faces] + lifted[faces:])
 
     first = stage(0)
-    rate_ref[...] = first
-    state_ref[...] = state_ref[...] + TIME_STEP * first
+    state = state_ref[...]
+    base_ref[...] = state + (0.5 * TIME_STEP) * first
+    state_ref[...] = state + TIME_STEP * first
     second = stage(1)
-    total = rate_ref[...] + second
-    for comp in range(6):
-        rows = slice(comp * elems, (comp + 1) * elems)
-        out_ref[:, comp, :] = fields_ref[:, comp, :] + 0.5 * TIME_STEP * total[rows]
+    out_ref[...] = base_ref[...] + (0.5 * TIME_STEP) * second
 
 
 def local(
@@ -375,39 +417,45 @@
     slot = wide_send.shape[3]
     faces = 6 * elems
     vmem = pl.BlockSpec(memory_space=pltpu.VMEM)
-    return pl.pallas_call(
+    hbm = pl.BlockSpec(memory_space=pltpu.HBM)
+    matrices = constants(elems)
+    result = pl.pallas_call(
         kernel,
-        out_shape=jax.ShapeDtypeStruct(fields.shape, fields.dtype),
-        in_specs=[vmem] * 15,
+        out_shape=jax.ShapeDtypeStruct((faces, 512), F32),
+        in_specs=[hbm] + [vmem] * 8 + [hbm] * 5 + [vmem],
         out_specs=vmem,
         scratch_shapes=[
             pltpu.VMEM((faces, 512), F32),
             pltpu.VMEM((faces, 512), F32),
+            *[pltpu.VMEM(matrix.shape, BF16) for matrix in matrices[:5]],
+            pltpu.VMEM((128, 128), F32),
             pltpu.VMEM((faces, 384), F32),
             pltpu.VMEM((faces, faces), BF16),
             pltpu.VMEM((faces, 6 * slot), BF16),
             pltpu.VMEM((6 * slot, faces), BF16),
-            pltpu.VMEM((3, faces, 128), F32),
+            pltpu.VMEM((4, faces, 128), F32),
             pltpu.VMEM((2, 6, slot, 384), F32),
             pltpu.VMEM((2, 6, slot, 384), F32),
+            pltpu.SemaphoreType.DMA((6,)),
             pltpu.SemaphoreType.DMA((2, 6)),
             pltpu.SemaphoreType.DMA((2, 6)),
         ],
         compiler_params=pltpu.CompilerParams(
-            collective_id=0, has_side_effects=True, vmem_limit_bytes=48 * 1024 * 1024
+            collective_id=0, has_side_effects=True, vmem_limit_bytes=67043328
         ),
     )(
-        fields,
-        scales,
-        class_table,
+        fields.transpose(1, 0, 2).reshape(faces, 512),
+        scales.T,
+        class_table.T,
         material.reshape(1, elems),
-        neighbour_class,
-        orientation,
-        face_source,
+        neighbour_class.T,
+        orientation.T,
+        face_source.T,
         wide_send,
         bulk_send,
-        *constants(elems),
+        *matrices,
     )
+    return result.reshape(6, elems, 512).transpose(1, 0, 2)
 
 
 def solution(mesh):

time: 28.9 us -> 22.4 us (0.78)
  local copies, waits for them, and re-layouts: 9.3 us -> 1.78 us
  Pallas kernels: 19.1 us -> 20.5 us
    unnamed x24 -> x1, local copies, waits for them, and re-layouts: 8.33 us -> 1.78 us
    pallas_call x1, Pallas kernels: 19.1 us -> 20.5 us  [local(): pl.pallas_call(kernel, out_shape=jax.ShapeDtypeStruct((faces, 512), F32),...]
    pallas_call x1 -> x0, local copies, waits for them, and re-layouts: 0.98 us -> none  [local(): pl.pallas_call(kernel, out_shape=jax.ShapeDtypeStruct(fields.shape, field...]
where the time goes in v2:
time: 22.4 us; the launch traced here: 22.2 us
  Pallas kernels  20.5 us (92%)
  local copies, waits for them, and re-layouts  1.78 us (8%)
    pallas_call x1, Pallas kernels, local(): pl.pallas_call(kernel, out_shape=jax.ShapeDtypeStruct((faces, 512), F32),...  20.5 us
    unnamed x1, local copies, waits for them, and re-layouts  1.78 us

profile of v2, /device:TPU:0, one launch (start us, length us, event | category | flops | bytes accessed | tf_op | source)
XLA Modules:
  0.0 22.2 jit_solution(4579033176782876110)
XLA Ops:
  0.0 20.5 %shard_map.145 = f32[192,512]{1,0:T(8,128)} custom-call(f32[192,512]{1,0:T(8,128)} %bitcast.13, f32[3,32]{1,0:T(4,128)} %bitcast.17, f32[2,8]{1,0:T(2,128)} %bitcast.18, s32[1,32]{1,0:T(1,128)} %bitcast.19, s32[6,32]{1,0:T(8,128)} %bitcast.14, s32[6,32]{1,0:T(8,128)} %bitcast.15, s32[6,32]{1,0:T(8,128)} %bitcast.16, s32[1,1,4,16]{3,2,1,0:T(4,128)} %wide_ref.1, ...), custom_call_target="tpu_custom_call" | custom-call | tf_op jit(solution)/shard_map/pallas_call | solution.py:422
  20.5 1.8 %copy.17 = f32[32,6,512]{2,0,1:T(8,128)} copy(f32[32,6,512]{2,0,1:T(8,128)} %bitcast.12) | data formatting | bytes 786432

commit v3 on v2

--- a/solution.py
+++ b/solution.py
@@ -75,7 +75,7 @@
     return high, low
 
 
-def constants(elems):
+def constants():
     pick = np.zeros((512, 384), dtype=np.float32)
     pick[face_nodes().reshape(-1), np.arange(384)] = 1.0
     turned = gll_numpy().T
@@ -98,16 +98,12 @@
                 turn[half * 64 + source, flag, half * 64 + place] = 1.0
     turn = turn.reshape(128, 1024)
     turn = np.concatenate([turn, turn], axis=0)
-    code = np.zeros((1, 6 * elems), dtype=np.float32)
-    for face in range(6):
-        code[0, face * elems : (face + 1) * elems] = 6 * np.arange(elems) + face
     return (
         jnp.asarray(pick, dtype=BF16),
         jnp.asarray(pick.T, dtype=BF16),
         jnp.asarray(d0),
         jnp.asarray(d12),
         jnp.asarray(turn, dtype=BF16),
-        jnp.asarray(code),
     )
 
 
@@ -134,6 +130,27 @@
 
 def kernel(
     fields_hbm,
+    scales_hbm,
+    class_hbm,
+    material_hbm,
+    neighbour_hbm,
+    orient_hbm,
+    source_hbm,
+    wide_hbm,
+    bulk_hbm,
+    pick_hbm,
+    lift_hbm,
+    d0_hbm,
+    d12_hbm,
+    turn_hbm,
+    out_ref,
+    state_ref,
+    base_ref,
+    pick_ref,
+    lift_ref,
+    d0_ref,
+    d12_ref,
+    turn_ref,
     scales_ref,
     class_ref,
     material_ref,
@@ -142,35 +159,22 @@
     source_ref,
     wide_ref,
     bulk_ref,
-    pick_hbm,
-    lift_hbm,
-    d0_hbm,
-    d12_hbm,
-    turn_hbm,
-    code_ref,
-    out_ref,
-    state_ref,
-    base_ref,
-    pick_ref,
-    lift_ref,
-    d0_ref,
-    d12_ref,
-    turn_ref,
     small_ref,
     table_ref,
     own_ref,
     far_ref,
     choose_ref,
     coef_ref,
+    curl_ref,
     send_ref,
     recv_ref,
     load_sem,
     send_sem,
     recv_sem,
 ):
-    elems = material_ref.shape[1]
+    elems = material_hbm.shape[1]
     faces = 6 * elems
-    slot = wide_ref.shape[3]
+    slot = wide_hbm.shape[3]
     wide_id, bulk_id = lax.axis_index("wide"), lax.axis_index("bulk")
     n_wide, n_bulk = lax.axis_size("wide"), lax.axis_size("bulk")
     targets = [(lax.rem(wide_id + offset + n_wide, n_wide), bulk_id) for offset in WIDE_OFFSETS]
@@ -181,22 +185,35 @@
     for target in targets:
         pl.semaphore_signal(barrier, inc=1, device_id=target, device_id_type=MESH)
 
-    loads = []
-    for place, (source, target) in enumerate(
+    loads = {}
+    for place, (name, source, target) in enumerate(
         (
-            (fields_hbm, state_ref),
-            (pick_hbm, pick_ref),
-            (d0_hbm, d0_ref),
-            (d12_hbm, d12_ref),
-            (turn_hbm, turn_ref),
-            (lift_hbm, lift_ref),
+            ("wide", wide_hbm, wide_ref),
+            ("bulk", bulk_hbm, bulk_ref),
+            ("fields", fields_hbm, state_ref),
+            ("pick", pick_hbm, pick_ref),
+            ("scales", scales_hbm, scales_ref),
+            ("class", class_hbm, class_ref),
+            ("material", material_hbm, material_ref),
+            ("neighbour", neighbour_hbm, neighbour_ref),
+            ("orient", orient_hbm, orient_ref),
+            ("source", source_hbm, source_ref),
+            ("d0", d0_hbm, d0_ref),
+            ("d12", d12_hbm, d12_ref),
+            ("turn", turn_hbm, turn_ref),
+            ("lift", lift_hbm, lift_ref),
         )
     ):
-        load = pltpu.make_async_copy(source, target, load_sem.at[place])
-        load.start()
-        loads.append(load)
-
-    code = code_ref[...]
+        loads[name] = pltpu.make_async_copy(source, target, load_sem.at[place])
+        loads[name].start()
+
+    spot = lax.broadcasted_iota(jnp.int32, (1, faces), 1)
+    part = jnp.zeros((1, faces), jnp.int32)
+    for face in range(1, 6):
+        part = part + jnp.where(spot >= face * elems, 1, 0)
+    code = (6 * (spot - elems * part) + part).astype(F32)
+    loads["wide"].wait()
+    loads["bulk"].wait()
     wide_rows = wide_ref[0, 0].astype(F32)
     bulk_rows = bulk_ref[0, 0].astype(F32)
     order = [wide_rows[q : q + 1] for q in range(4)] + [bulk_rows[1:2], bulk_rows[0:1]]
@@ -204,58 +221,62 @@
         choose_ref[q * slot : (q + 1) * slot, :] = jnp.where(column(row) == code, 1.0, 0.0).astype(BF16)
 
     low_half = lax.broadcasted_iota(jnp.int32, (elems, 128), 1) < 64
-    far_code = (lax.broadcasted_iota(jnp.int32, (elems, 6 * slot), 1) + faces).astype(F32)
-    material = material_ref[...]
-    neighbour = neighbour_ref[...]
-    table = class_ref[...]
-    imped = jnp.sqrt(table[1:2, :] / table[0:1, :])
-    permit = jnp.zeros((1, elems), F32)
-    permea = jnp.zeros((1, elems), F32)
-    own_imp = jnp.zeros((1, elems), F32)
-    z_out = jnp.zeros((6, elems), F32)
-    for entry in range(class_ref.shape[1]):
-        hit = material == entry
-        permit = permit + jnp.where(hit, table[0:1, entry : entry + 1], 0.0)
-        permea = permea + jnp.where(hit, table[1:2, entry : entry + 1], 0.0)
-        own_imp = own_imp + jnp.where(hit, imped[:, entry : entry + 1], 0.0)
-        z_out = z_out + jnp.where(neighbour == entry, imped[:, entry : entry + 1], 0.0)
-    side = lax.broadcasted_iota(jnp.int32, (6, elems), 0)
-    sign = jnp.where((side & 1) > 0, 1.0, -1.0)
-    scales = scales_ref[...]
-    lift = LIFT_WEIGHT * jnp.where(side < 2, scales[0:1], jnp.where(side < 4, scales[1:2], scales[2:3]))
-    e_factor = -lift / (permit * (own_imp + z_out))
-    h_factor = lift / (permea * (1.0 / own_imp + 1.0 / z_out))
-    small_ref[...] = jnp.zeros_like(small_ref)
-    small_ref[0:6, 0:elems] = source_ref[...].astype(F32)
-    small_ref[8:14, 0:elems] = orient_ref[...].astype(F32)
-    small_ref[16:22, 0:elems] = e_factor
-    small_ref[24:30, 0:elems] = -h_factor
-    small_ref[32:38, 0:elems] = -sign * z_out * e_factor
-    small_ref[40:46, 0:elems] = -sign * h_factor / z_out
-    small_ref[48:51, 0:elems] = scales / permit
-    small_ref[56:59, 0:elems] = -scales / permea
-    columns = jnp.transpose(small_ref[...])[0:elems]
-
-    def col(group, index):
-        return columns[:, 8 * group + index : 8 * group + index + 1]
-
-    flags = []
-    for face in range(6):
-        rows = slice(face * elems, (face + 1) * elems)
-        origin = col(0, face)
-        own_ref[rows, :] = jnp.where(origin == code, 1.0, 0.0).astype(BF16)
-        far_ref[rows, :] = jnp.where(origin == far_code, 1.0, 0.0).astype(BF16)
-        coef_ref[0, rows, :] = jnp.where(low_half, col(2, face), col(3, face))
-        coef_ref[1, rows, :] = jnp.where(low_half, col(4, face), col(5, face))
-        coef_ref[2, rows, :] = jnp.where(origin < 0.0, jnp.where(low_half, 2.0, 0.0), 1.0)
-        coef_ref[3, rows, :] = jnp.broadcast_to(col(1, face), (elems, 128))
-
-    pl.semaphore_wait(barrier, len(targets))
+
+    def prepare():
+        for name in ("scales", "class", "material", "neighbour", "orient", "source"):
+            loads[name].wait()
+        far_code = (lax.broadcasted_iota(jnp.int32, (elems, 6 * slot), 1) + faces).astype(F32)
+        material = material_ref[...]
+        neighbour = neighbour_ref[...]
+        table = class_ref[...]
+        imped = jnp.sqrt(table[1:2, :] / table[0:1, :])
+        permit = jnp.zeros((1, elems), F32)
+        permea = jnp.zeros((1, elems), F32)
+        own_imp = jnp.zeros((1, elems), F32)
+        z_out = jnp.zeros((6, elems), F32)
+        for entry in range(class_ref.shape[1]):
+            hit = material == entry
+            permit = permit + jnp.where(hit, table[0:1, entry : entry + 1], 0.0)
+            permea = permea + jnp.where(hit, table[1:2, entry : entry + 1], 0.0)
+            own_imp = own_imp + jnp.where(hit, imped[:, entry : entry + 1], 0.0)
+            z_out = z_out + jnp.where(neighbour == entry, imped[:, entry : entry + 1], 0.0)
+        side = lax.broadcasted_iota(jnp.int32, (6, elems), 0)
+        sign = jnp.where((side & 1) > 0, 1.0, -1.0)
+        scales = scales_ref[...]
+        lift = LIFT_WEIGHT * jnp.where(side < 2, scales[0:1], jnp.where(side < 4, scales[1:2], scales[2:3]))
+        e_factor = -lift / (permit * (own_imp + z_out))
+        h_factor = lift / (permea * (1.0 / own_imp + 1.0 / z_out))
+        small_ref[...] = jnp.zeros_like(small_ref)
+        small_ref[0:6, 0:elems] = source_ref[...].astype(F32)
+        small_ref[8:14, 0:elems] = orient_ref[...].astype(F32)
+        small_ref[16:22, 0:elems] = e_factor
+        small_ref[24:30, 0:elems] = -h_factor
+        small_ref[32:38, 0:elems] = -sign * z_out * e_factor
+        small_ref[40:46, 0:elems] = -sign * h_factor / z_out
+        small_ref[48:51, 0:elems] = scales / permit
+        small_ref[56:59, 0:elems] = -scales / permea
+        columns = jnp.transpose(small_ref[...])[0:elems]
+
+        def col(group, index):
+            return columns[:, 8 * group + index : 8 * group + index + 1]
+
+        for face in range(6):
+            rows = slice(face * elems, (face + 1) * elems)
+            origin = col(0, face)
+            own_ref[rows, :] = jnp.where(origin == code, 1.0, 0.0).astype(BF16)
+            far_ref[rows, :] = jnp.where(origin == far_code, 1.0, 0.0).astype(BF16)
+            coef_ref[0, rows, :] = jnp.where(low_half, col(2, face), col(3, face))
+            coef_ref[1, rows, :] = jnp.where(low_half, col(4, face), col(5, face))
+            coef_ref[2, rows, :] = jnp.where(origin < 0.0, jnp.where(low_half, 2.0, 0.0), 1.0)
+            coef_ref[3, rows, :] = jnp.broadcast_to(col(1, face), (elems, 128))
+        for axis in range(3):
+            curl_ref[0, axis] = jnp.broadcast_to(col(6, axis), (elems, 128))
+            curl_ref[1, axis] = jnp.broadcast_to(col(7, axis), (elems, 128))
 
     def stage(number):
         if number == 0:
-            loads[0].wait()
-            loads[1].wait()
+            loads["fields"].wait()
+            loads["pick"].wait()
         high, low = split(state_ref[...])
         both = mul(jnp.concatenate([high, low], axis=0), pick_ref[...])
         traces = both[0:faces] + both[faces:]
@@ -277,6 +298,8 @@
         copies = []
         for q, target in enumerate(targets):
             send_ref[number, q] = sent[q * slot : (q + 1) * slot]
+        if number == 0:
+            pl.semaphore_wait(barrier, len(targets))
         for q, target in enumerate(targets):
             copy = pltpu.make_async_remote_copy(
                 src_ref=send_ref.at[number, q],
@@ -290,8 +313,9 @@
             copies.append(copy)
 
         if number == 0:
-            loads[2].wait()
-            loads[3].wait()
+            prepare()
+            loads["d0"].wait()
+            loads["d12"].wait()
         active = jnp.concatenate([high[elems : 3 * elems], high[4 * elems :]], axis=0)
         active_low = jnp.concatenate([low[elems : 3 * elems], low[4 * elems :]], axis=0)
         slope0 = mul(jnp.concatenate([active, active_low], axis=0), d0_ref[0])
@@ -318,21 +342,24 @@
                 axis=1,
             )
 
+        def factor(field, axis):
+            return jnp.concatenate([curl_ref[field, axis]] * 4, axis=1)
+
         volume = []
         for field in range(2):
             other = 3 * (1 - field)
             for dim in range(3):
                 one, two = (dim + 1) % 3, (dim + 2) % 3
                 volume.append(
-                    col(6 + field, one) * slope(other + two, one)
-                    - col(6 + field, two) * slope(other + one, two)
+                    factor(field, one) * slope(other + two, one)
+                    - factor(field, two) * slope(other + one, two)
                 )
         volume = jnp.concatenate(volume, axis=0)
 
         got = mul(own_ref[...], tab)
         if number == 0:
-            loads[4].wait()
-            loads[5].wait()
+            loads["turn"].wait()
+            loads["lift"].wait()
         for copy in copies:
             copy.wait()
         beyond = jnp.concatenate(split(recv_ref[number].reshape(6 * slot, 384)), axis=1)
@@ -418,32 +445,8 @@
     faces = 6 * elems
     vmem = pl.BlockSpec(memory_space=pltpu.VMEM)
     hbm = pl.BlockSpec(memory_space=pltpu.HBM)
-    matrices = constants(elems)
-    result = pl.pallas_call(
-        kernel,
-        out_shape=jax.ShapeDtypeStruct((faces, 512), F32),
-        in_specs=[hbm] + [vmem] * 8 + [hbm] * 5 + [vmem],
-        out_specs=vmem,
-        scratch_shapes=[
-            pltpu.VMEM((faces, 512), F32),
-            pltpu.VMEM((faces, 512), F32),
-            *[pltpu.VMEM(matrix.shape, BF16) for matrix in matrices[:5]],
-            pltpu.VMEM((128, 128), F32),
-            pltpu.VMEM((faces, 384), F32),
-            pltpu.VMEM((faces, faces), BF16),
-            pltpu.VMEM((faces, 6 * slot), BF16),
-            pltpu.VMEM((6 * slot, faces), BF16),
-            pltpu.VMEM((4, faces, 128), F32),
-            pltpu.VMEM((2, 6, slot, 384), F32),
-            pltpu.VMEM((2, 6, slot, 384), F32),
-            pltpu.SemaphoreType.DMA((6,)),
-            pltpu.SemaphoreType.DMA((2, 6)),
-            pltpu.SemaphoreType.DMA((2, 6)),
-        ],
-        compiler_params=pltpu.CompilerParams(
-            collective_id=0, has_side_effects=True, vmem_limit_bytes=67043328
-        ),
-    )(
+    matrices = constants()
+    arguments = (
         fields.transpose(1, 0, 2).reshape(faces, 512),
         scales.T,
         class_table.T,
@@ -453,8 +456,34 @@
         face_source.T,
         wide_send,
         bulk_send,
-        *matrices,
     )
+    result = pl.pallas_call(
+        kernel,
+        out_shape=jax.ShapeDtypeStruct((faces, 512), F32),
+        in_specs=[hbm] * 14,
+        out_specs=vmem,
+        scratch_shapes=[
+            pltpu.VMEM((faces, 512), F32),
+            pltpu.VMEM((faces, 512), F32),
+            *[pltpu.VMEM(matrix.shape, BF16) for matrix in matrices],
+            *[pltpu.VMEM(value.shape, value.dtype) for value in arguments[1:]],
+            pltpu.VMEM((128, 128), F32),
+            pltpu.VMEM((faces, 384), F32),
+            pltpu.VMEM((faces, faces), BF16),
+            pltpu.VMEM((faces, 6 * slot), BF16),
+            pltpu.VMEM((6 * slot, faces), BF16),
+            pltpu.VMEM((4, faces, 128), F32),
+            pltpu.VMEM((2, 3, elems, 128), F32),
+            pltpu.VMEM((2, 6, slot, 384), F32),
+            pltpu.VMEM((2, 6, slot, 384), F32),
+            pltpu.SemaphoreType.DMA((14,)),
+            pltpu.SemaphoreType.DMA((2, 6)),
+            pltpu.SemaphoreType.DMA((2, 6)),
+        ],
+        compiler_params=pltpu.CompilerParams(
+            collective_id=0, has_side_effects=True, vmem_limit_bytes=67043328
+        ),
+    )(*arguments, *matrices)
     return result.reshape(6, elems, 512).transpose(1, 0, 2)
 
 

time: 22.4 us -> 21 us (0.938)
  Pallas kernels: 20.5 us -> 19.1 us
    pallas_call x1, Pallas kernels: 20.5 us -> 19.1 us  [local(): pl.pallas_call(kernel, out_shape=jax.ShapeDtypeStruct((faces, 512), F32),...]
where the time goes in v3:
time: 21 us; the launch traced here: 20.8 us
  Pallas kernels  19.1 us (91%)
  local copies, waits for them, and re-layouts  1.78 us (8%)
    pallas_call x1, Pallas kernels, local(): pl.pallas_call(kernel, out_shape=jax.ShapeDtypeStruct((faces, 512), F32),...  19.1 us
    unnamed x1, local copies, waits for them, and re-layouts  1.78 us

profile of v3, /device:TPU:0, one launch (start us, length us, event | category | flops | bytes accessed | tf_op | source)
XLA Modules:
  0.0 20.8 jit_solution(15532394109596293322)
XLA Ops:
  0.0 19.1 %shard_map.136 = f32[192,512]{1,0:T(8,128)} custom-call(f32[192,512]{1,0:T(8,128)} %bitcast.13, f32[3,32]{1,0:T(4,128)} %bitcast.17, f32[2,8]{1,0:T(2,128)} %bitcast.18, s32[1,32]{1,0:T(1,128)} %bitcast.19, s32[6,32]{1,0:T(8,128)} %bitcast.14, s32[6,32]{1,0:T(8,128)} %bitcast.15, s32[6,32]{1,0:T(8,128)} %bitcast.16, s32[1,1,4,16]{3,2,1,0:T(4,128)} %wide_hbm.1, ...), custom_call_target="tpu_custom_call" | custom-call | tf_op jit(solution)/shard_map/pallas_call | solution.py:460
  19.1 1.8 %copy.16 = f32[32,6,512]{2,0,1:T(8,128)} copy(f32[32,6,512]{2,0,1:T(8,128)} %bitcast.12) | data formatting | bytes 786432

commit v4 on v3

--- a/solution.py
+++ b/solution.py
@@ -481,9 +481,9 @@
             pltpu.SemaphoreType.DMA((2, 6)),
         ],
         compiler_params=pltpu.CompilerParams(
-            collective_id=0, has_side_effects=True, vmem_limit_bytes=67043328
+            collective_id=0, has_side_effects=True, vmem_limit_bytes=48 * 1024 * 1024
         ),
-    )(*arguments, *matrices)
+    )(*[pltpu.with_memory_space_constraint(value, pltpu.HBM) for value in (*arguments, *matrices)])
     return result.reshape(6, elems, 512).transpose(1, 0, 2)
 
 

time: 21 us -> 19.2 us (0.914)
  local copies, waits for them, and re-layouts: 1.78 us -> 0.75 us
  Pallas kernels: 19.1 us -> 18.3 us
    unnamed x1, local copies, waits for them, and re-layouts: 1.78 us -> 0.75 us
    pallas_call x1, Pallas kernels: 19.1 us -> 18.3 us  [local(): pl.pallas_call(kernel, out_shape=jax.ShapeDtypeStruct((faces, 512), F32),...]
where the time goes in v4:
time: 19.2 us; the launch traced here: 19.1 us
  Pallas kernels  18.3 us (95%)
  local copies, waits for them, and re-layouts  0.75 us (4%)
    pallas_call x1, Pallas kernels, local(): pl.pallas_call(kernel, out_shape=jax.ShapeDtypeStruct((faces, 512), F32),...  18.3 us
    unnamed x1, local copies, waits for them, and re-layouts  0.75 us

profile of v4, /device:TPU:0, one launch (start us, length us, event | category | flops | bytes accessed | tf_op | source)
XLA Modules:
  0.0 19.1 jit_solution(8970303112646214431)
XLA Ops:
  0.0 18.3 %shard_map.136 = f32[192,512]{1,0:T(8,128)S(1)} custom-call(f32[192,512]{1,0:T(8,128)} %bitcast.13, f32[3,32]{1,0:T(4,128)} %bitcast.17, f32[2,8]{1,0:T(2,128)} %bitcast.18, s32[1,32]{1,0:T(1,128)} %bitcast.19, s32[6,32]{1,0:T(8,128)} %bitcast.14, s32[6,32]{1,0:T(8,128)} %bitcast.15, s32[6,32]{1,0:T(8,128)} %bitcast.16, s32[1,1,4,16]{3,2,1,0:T(4,128)} %wide_hbm.1, ...), custom_call_target="tpu_custom_call" | custom-call | tf_op jit(solution)/shard_map/pallas_call | solution.py:460
  18.3 0.7 %copy.16 = f32[32,6,512]{2,0,1:T(8,128)} copy(f32[32,6,512]{2,0,1:T(8,128)S(1)} %bitcast.12) | data formatting | bytes 786432

commit v5 on v4

--- a/solution.py
+++ b/solution.py
@@ -99,8 +99,8 @@
     turn = turn.reshape(128, 1024)
     turn = np.concatenate([turn, turn], axis=0)
     return (
-        jnp.asarray(pick, dtype=BF16),
-        jnp.asarray(pick.T, dtype=BF16),
+        jnp.asarray(pick[:, 128:], dtype=BF16),
+        jnp.asarray(pick[:, 128:].T, dtype=BF16),
         jnp.asarray(d0),
         jnp.asarray(d12),
         jnp.asarray(turn, dtype=BF16),
@@ -205,7 +205,8 @@
         )
     ):
         loads[name] = pltpu.make_async_copy(source, target, load_sem.at[place])
-        loads[name].start()
+        if name not in ("d0", "d12", "turn", "lift"):
+            loads[name].start()
 
     spot = lax.broadcasted_iota(jnp.int32, (1, faces), 1)
     part = jnp.zeros((1, faces), jnp.int32)
@@ -277,9 +278,14 @@
         if number == 0:
             loads["fields"].wait()
             loads["pick"].wait()
-        high, low = split(state_ref[...])
+            for name in ("d0", "d12", "turn", "lift"):
+                loads[name].start()
+        state = state_ref[...]
+        high, low = split(state)
         both = mul(jnp.concatenate([high, low], axis=0), pick_ref[...])
-        traces = both[0:faces] + both[faces:]
+        every = lax.broadcasted_iota(jnp.int32, (faces, 128), 1) < 64
+        ends = jnp.where(every, state[:, 0:128], state[:, 384:512])
+        traces = jnp.concatenate([ends, both[0:faces] + both[faces:]], axis=1)
         half = lax.broadcasted_iota(jnp.int32, (3 * elems, 128), 1) < 64
         for axis in range(3):
             e_part = traces[0 : 3 * elems, axis * 128 : (axis + 1) * 128]
@@ -300,7 +306,8 @@
             send_ref[number, q] = sent[q * slot : (q + 1) * slot]
         if number == 0:
             pl.semaphore_wait(barrier, len(targets))
-        for q, target in enumerate(targets):
+        for q in (1, 2, 0, 3, 4, 5):
+            target = targets[q]
             copy = pltpu.make_async_remote_copy(
                 src_ref=send_ref.at[number, q],
                 dst_ref=recv_ref.at[number, q],
@@ -418,8 +425,12 @@
                     else:
                         line.append(jnp.where(low_half, swap(near), away))
                 lines.append(jnp.concatenate(line, axis=1))
-        lifted = mul(jnp.concatenate(split(jnp.concatenate(lines, axis=0)), axis=0), lift_ref[...])
-        return volume + (lifted[0:faces] + lifted[faces:])
+        lines = jnp.concatenate(lines, axis=0)
+        lifted = mul(jnp.concatenate(split(lines[:, 128:]), axis=0), lift_ref[...])
+        ends = lines[:, 0:128]
+        none = jnp.zeros_like(ends)
+        ends = jnp.concatenate([jnp.where(every, ends, 0.0), none, none, jnp.where(every, 0.0, ends)], axis=1)
+        return volume + ends + (lifted[0:faces] + lifted[faces:])
 
     first = stage(0)
     state = state_ref[...]

time: 19.2 us -> 18.5 us (0.964)
  Pallas kernels: 18.3 us -> 17.6 us
    pallas_call x1, Pallas kernels: 18.3 us -> 17.6 us  [local(): pl.pallas_call(kernel, out_shape=jax.ShapeDtypeStruct((faces, 512), F32),...]
where the time goes in v5:
time: 18.5 us; the launch traced here: 18.3 us
  Pallas kernels  17.6 us (95%)
  local copies, waits for them, and re-layouts  0.75 us (4%)
    pallas_call x1, Pallas kernels, local(): pl.pallas_call(kernel, out_shape=jax.ShapeDtypeStruct((faces, 512), F32),...  17.6 us
    unnamed x1, local copies, waits for them, and re-layouts  0.75 us

profile of v5, /device:TPU:0, one launch (start us, length us, event | category | flops | bytes accessed | tf_op | source)
XLA Modules:
  0.0 18.3 jit_solution(17643536350914617055)
XLA Ops:
  0.0 17.6 %shard_map.136 = f32[192,512]{1,0:T(8,128)S(1)} custom-call(f32[192,512]{1,0:T(8,128)} %bitcast.13, f32[3,32]{1,0:T(4,128)} %bitcast.17, f32[2,8]{1,0:T(2,128)} %bitcast.18, s32[1,32]{1,0:T(1,128)} %bitcast.19, s32[6,32]{1,0:T(8,128)} %bitcast.14, s32[6,32]{1,0:T(8,128)} %bitcast.15, s32[6,32]{1,0:T(8,128)} %bitcast.16, s32[1,1,4,16]{3,2,1,0:T(4,128)} %wide_hbm.1, ...), custom_call_target="tpu_custom_call" | custom-call | tf_op jit(solution)/shard_map/pallas_call | solution.py:471
  17.6 0.7 %copy.16 = f32[32,6,512]{2,0,1:T(8,128)} copy(f32[32,6,512]{2,0,1:T(8,128)S(1)} %bitcast.12) | data formatting | bytes 786432
